TPU v7x, 256 devices: a whole 4x4x8 slice. The times are simulated.
256 devices in a mesh: ka: 8 (over y_lo, x), pw: 32 (over y_hi, z, core).
Axes of the slice: x: 4, y: 4 (y_hi: 2, y_lo: 2; y = y_hi * 2 + y_lo), z: 8, core: 2. Of those that a mesh axis runs over, the one named last changes fastest.
Arguments:
- states_re: bfloat16 [16, 512, 32768], P('ka', None, 'pw'), may hold values from -0.016572815 to 0.016572815
- states_im: bfloat16 [16, 512, 32768], P('ka', None, 'pw'), may hold values from -0.016572815 to 0.016572815
Outputs:
- wilson_lines: float32 [16, 512, 2, 512], P('ka', 'pw')
All inputs are finite; a program needn't handle non-finite values.
Results may differ from a plain program's by a relative error of at most 0.0003.
Values may be sent and summed in bfloat16 or wider, within the bound.
A program may use at most 64 MiB of HBM per device.

v0:
```python
import jax
import jax.numpy as jnp
from jax import lax
from jax.sharding import PartitionSpec as P


def from_behind(block, axis, distance):
    devices = range(lax.axis_size(axis))
    route = [((i - distance) % len(devices), i) for i in devices]
    return lax.ppermute(block, axis, route)


def shifted(shard, axis, by):
    size = lax.axis_size(axis)
    pairs = [(i, i + by) for i in range(size) if 0 <= i + by < size]
    return lax.ppermute(shard, axis, pairs)


def complex_rows(left, right):
    highest = lax.Precision.HIGHEST
    left_re = left[:, 0]
    left_im = left[:, 1]
    right_re = right[:, 0]
    right_im = right[:, 1]
    real_part = jnp.dot(
        left_re, right_re, precision=highest, preferred_element_type=jnp.float32
    ) - jnp.dot(left_im, right_im, precision=highest, preferred_element_type=jnp.float32)
    imag_part = jnp.dot(
        left_re, right_im, precision=highest, preferred_element_type=jnp.float32
    ) + jnp.dot(left_im, right_re, precision=highest, preferred_element_type=jnp.float32)
    return jnp.stack([real_part, imag_part], 1)


def shards(states_re, states_im):
    kcount = states_re.shape[0]
    bands = states_re.shape[1]
    pw_width = lax.axis_size("pw")
    ka_width = lax.axis_size("ka")
    band_rows = bands // pw_width
    ka_place = lax.axis_index("ka")
    first_band = lax.axis_index("pw") * band_rows
    next_re, next_im = from_behind((states_re[:1], states_im[:1]), "ka", -1)
    after_re = jnp.concatenate([states_re[1:], next_re], 0)
    after_im = jnp.concatenate([states_im[1:], next_im], 0)
    real_part = jnp.einsum(
        "kbg,kcg->bkc", states_re, after_re, preferred_element_type=jnp.float32
    ) + jnp.einsum("kbg,kcg->bkc", states_im, after_im, preferred_element_type=jnp.float32)
    imag_part = jnp.einsum(
        "kbg,kcg->bkc", states_re, after_im, preferred_element_type=jnp.float32
    ) - jnp.einsum("kbg,kcg->bkc", states_im, after_re, preferred_element_type=jnp.float32)
    margin_rows = lax.psum_scatter(
        jnp.stack([real_part, imag_part], 2), "pw", scatter_dimension=0, tiled=True
    )
    margin_full = lax.all_gather(margin_rows, "pw", axis=0, tiled=True)
    row_index = lax.broadcasted_iota(jnp.int32, (band_rows, bands), 0) + first_band
    col_index = lax.broadcasted_iota(jnp.int32, (band_rows, bands), 1)
    eye_real = (row_index == col_index).astype(jnp.float32)
    eye_rows = jnp.stack([eye_real, jnp.zeros_like(eye_real)], 1)

    def sweep(start_rows):
        current = start_rows
        collected = []
        for kpoint in range(kcount):
            current = complex_rows(current, margin_full[:, kpoint])
            collected.append(current)
        return jnp.stack(collected, 0)

    own_span = sweep(eye_rows)[-1]
    span_whole = lax.all_gather(own_span, "pw", axis=0, tiled=True)

    def advance(position, start_rows):
        last_line = complex_rows(start_rows, span_whole)
        received = shifted(last_line, "ka", 1)
        return jnp.where(ka_place == position + 1, received, start_rows)

    start_rows = lax.fori_loop(0, ka_width - 1, advance, eye_rows)
    return sweep(start_rows)


def solution(mesh):
    in_specs = (P("ka", None, "pw"), P("ka", None, "pw"))
    out_specs = P("ka", "pw", None, None)
    return jax.shard_map(shards, mesh=mesh, in_specs=in_specs, out_specs=out_specs, check_vma=False)
```

profile of v0, /device:TPU:14, one launch (start us, length us, event | category | flops | bytes accessed | tf_op | source)
XLA Modules:
  0.0 625.4 jit_solution(6827714051969218923)
XLA Ops:
  6.5 1.9 fusion.87
  10.1 26.5 %collective-permute-done.2 = bf16[1,512,1024]{2,1,0:T(8,128)(2,1)S(1)} collective-permute-done((bf16[1,512,1024]{2,1,0:T(8,128)(2,1)S(1)}, bf16[1,512,1024]{2,1,0:T(8,128)(2,1)S(1)}, u32[]{:S(2)}, u32[]{:S(2)}) %collective-permute-start.2) | collective-permute-done | bytes 1048608 | tf_op jit(solution)/shard_map/ppermute | solution.py:10
  37.9 20.1 %collective-permute-done.1 = bf16[1,512,1024]{2,1,0:T(8,128)(2,1)S(1)} collective-permute-done((bf16[1,512,1024]{2,1,0:T(8,128)(2,1)S(1)}, bf16[1,512,1024]{2,1,0:T(8,128)(2,1)S(1)}, u32[]{:S(2)}, u32[]{:S(2)}) %collective-permute-start.1) | collective-permute-done | bytes 1048608 | tf_op jit(solution)/shard_map/ppermute | solution.py:10
  61.8 2.4 pad_maximum_fusion.1
  64.3 7.3 %copy.5 = f32[512,2,2,512]{3,2,1,0:T(2,128)} copy(f32[512,2,2,512]{0,3,1,2:T(8,128)} %pad_maximum_fusion.1) | data formatting | bytes 8388608 | tf_op jit(solution)/shard_map/stack | solution.py:52
  73.5 279.7 %all-reduce.4.cloned.1.call-done = f32[512,2,2,512]{3,2,1,0:T(2,128)} async-done(((f32[512,2,2,512]{3,2,1,0:T(2,128)}), f32[512,2,2,512]{3,2,1,0:T(2,128)}) %all-reduce.4.cloned.1.call-update) | async-done | bytes 4194320
  354.9 86.2 %all-gather.3.cloned.1.call-done = f32[512,2,2,512]{3,2,1,0:T(2,128)} async-done(((f32[16,2,2,512]{3,2,1,0:T(2,128)}), f32[512,2,2,512]{3,2,1,0:T(2,128)}) %all-gather.3.cloned.1.call-update) | async-done | bytes 4194320 | tf_op jit(solution)/shard_map/all_gather | solution.py:54
  441.2 3.7 slice_bitcast_fusion
  444.8 3.5 fusion.85
  453.7 76.6 %all-gather.5.cloned.1.call-done = f32[512,2,512]{2,0,1:T(8,128)} async-done(((f32[16,2,512]{2,0,1:T(8,128)}), f32[512,2,512]{2,0,1:T(8,128)}) %all-gather.5.cloned.1.call-update) | async-done | bytes 2097168 | tf_op jit(solution)/shard_map/all_gather | solution.py:69
  530.3 3.2 copy.6
  533.5 76.8 %while.13 = (s32[]{:T(128)}, f32[16,2,512]{2,0,1:T(8,128)S(1)}, s32[]{:T(128)}, f32[512,2,512]{2,1,0:T(2,128)S(1)}, s32[]{:T(128)}) while((s32[]{:T(128)}, f32[16,2,512]{2,0,1:T(8,128)S(1)}, s32[]{:T(128)}, f32[512,2,512]{2,1,0:T(2,128)S(1)}, s32[]{:T(128)}) %tuple.40), condition=%wide.region_2.3_spmd, body=%wide.region_1.2_spmd.sunk | while | flops 201375744 | bytes 9306223 | solution.py:76
  539.0 4.9 collective-permute-done
  543.8 1.6 fusion.122
  549.3 4.9 collective-permute-done
  559.6 4.9 collective-permute-done
  569.9 4.9 collective-permute-done
  574.8 1.6 fusion.122
  580.2 5.0 collective-permute-done
  590.7 7.0 %collective-permute-done = f32[16,2,512]{2,0,1:T(8,128)S(1)} collective-permute-done((f32[16,2,512]{2,0,1:T(8,128)S(1)}, f32[16,2,512]{2,0,1:T(8,128)S(1)}, u32[]{:S(2)}, u32[]{:S(2)}) %collective-permute-start) | collective-permute-done | bytes 65568 | tf_op jit(solution)/shard_map/while/body/eval_jaxpr/ppermute | solution.py:16
  597.7 1.6 fusion.122
  603.1 7.0 %collective-permute-done = f32[16,2,512]{2,0,1:T(8,128)S(1)} collective-permute-done((f32[16,2,512]{2,0,1:T(8,128)S(1)}, f32[16,2,512]{2,0,1:T(8,128)S(1)}, u32[]{:S(2)}, u32[]{:S(2)}) %collective-permute-start) | collective-permute-done | bytes 65568 | tf_op jit(solution)/shard_map/while/body/eval_jaxpr/ppermute | solution.py:16
  610.4 2.0 fusion.38
  612.4 1.9 fusion.45
  (108 shorter events, 52.7 us)
Async XLA Ops:
  6.5 2.8 copy-start.7
  6.5 346.7 %all-reduce.4.cloned.1.call-start = ((), (), s32[]{:S(2)}) async-start(), calls=%async_computation.2 | async-start | bytes 8388608
  8.4 28.2 %copy-start.6 = (bf16[2,512,1024]{2,1,0:T(8,128)(2,1)S(1)}, bf16[2,512,1024]{2,1,0:T(8,128)(2,1)}, u32[]{:S(2)}) copy-start(bf16[2,512,1024]{2,1,0:T(8,128)(2,1)} %param.5) | copy-start | bytes 6291460
  8.4 28.2 %collective-permute-start.2 = (bf16[1,512,1024]{2,1,0:T(8,128)(2,1)S(1)}, bf16[1,512,1024]{2,1,0:T(8,128)(2,1)S(1)}, u32[]{:S(2)}, u32[]{:S(2)}) collective-permute-start(bf16[1,512,1024]{2,1,0:T(8,128)(2,1)S(1)} %get-tuple-element.110), channel_id=1, source_target_pairs={{32,0},{64,32},{96,64},{128,96},{160,128},{192,160},{224,192},{0,2... | collective-permute-start | bytes 3145736 | tf_op jit(solution)/shard_map/ppermute | solution.py:10
  9.5 48.5 %collective-permute-start.1 = (bf16[1,512,1024]{2,1,0:T(8,128)(2,1)S(1)}, bf16[1,512,1024]{2,1,0:T(8,128)(2,1)S(1)}, u32[]{:S(2)}, u32[]{:S(2)}) collective-permute-start(bf16[1,512,1024]{2,1,0:T(8,128)(2,1)S(1)} %get-tuple-element.112), channel_id=1, source_target_pairs={{32,0},{64,32},{96,64},{128,96},{160,128},{192,160},{224,192},{0,2... | collective-permute-start | bytes 3145736 | tf_op jit(solution)/shard_map/ppermute | solution.py:10
  71.6 0.7 copy-start.8
  71.6 369.5 %all-gather.3.cloned.1.call-start = ((), (), s32[]{:S(2)}) async-start(), calls=%async_computation | async-start | bytes 4325376 | tf_op jit(solution)/shard_map/all_gather | solution.py:54
  354.9 175.4 %all-gather.5.cloned.1.call-start = ((), (), s32[]{:S(2)}) async-start(), calls=%async_computation.1 | async-start | bytes 2162688 | tf_op jit(solution)/shard_map/all_gather | solution.py:69
  448.3 2.2 copy-start.2
  448.3 2.2 copy-start.4
  448.3 3.4 copy-start
  537.7 6.2 collective-permute-start
  548.0 6.2 collective-permute-start
  558.3 6.2 collective-permute-start
  568.6 6.2 collective-permute-start
  578.9 6.3 %collective-permute-start = (f32[16,2,512]{2,0,1:T(8,128)S(1)}, f32[16,2,512]{2,0,1:T(8,128)S(1)}, u32[]{:S(2)}, u32[]{:S(2)}) collective-permute-start(f32[16,2,512]{2,0,1:T(8,128)S(1)} %pad_maximum_fusion.11), channel_id=1, source_target_pairs={{0,32},{32,64},{64,96},{96,128},{128,160},{160,192},{192,224},{1,3... | collective-permute-start | bytes 196616 | tf_op jit(solution)/shard_map/while/body/eval_jaxpr/ppermute | solution.py:16
  589.4 8.3 %collective-permute-start = (f32[16,2,512]{2,0,1:T(8,128)S(1)}, f32[16,2,512]{2,0,1:T(8,128)S(1)}, u32[]{:S(2)}, u32[]{:S(2)}) collective-permute-start(f32[16,2,512]{2,0,1:T(8,128)S(1)} %pad_maximum_fusion.11), channel_id=1, source_target_pairs={{0,32},{32,64},{64,96},{96,128},{128,160},{160,192},{192,224},{1,3... | collective-permute-start | bytes 196616 | tf_op jit(solution)/shard_map/while/body/eval_jaxpr/ppermute | solution.py:16
  601.8 8.3 %collective-permute-start = (f32[16,2,512]{2,0,1:T(8,128)S(1)}, f32[16,2,512]{2,0,1:T(8,128)S(1)}, u32[]{:S(2)}, u32[]{:S(2)}) collective-permute-start(f32[16,2,512]{2,0,1:T(8,128)S(1)} %pad_maximum_fusion.11), channel_id=1, source_target_pairs={{0,32},{32,64},{64,96},{96,128},{128,160},{160,192},{192,224},{1,3... | collective-permute-start | bytes 196616 | tf_op jit(solution)/shard_map/while/body/eval_jaxpr/ppermute | solution.py:16
  610.3 3.9 copy-start.5
  610.3 5.2 copy-start.1
  612.4 3.8 copy-start.3
Sparse Core Ops, SparseCore 0:
  71.8 281.4 all-reduce.3
  356.0 85.0 all-gather.2
  453.8 76.5 all-gather.4
where the time goes:
time: 636 us; the launch traced here: 625 us
  waiting for transfers between devices  527 us (83%)
  matrix products  34.8 us (5%)
  local copies, waits for them, and re-layouts  34.6 us (5%)
  between operations  13.9 us (2%)
  starting transfers between devices  10.6 us (2%)
    unnamed x4, waiting for transfers between devices  280 us
    all_gather x1, waiting for transfers between devices, shards(): margin_full = lax.all_gather(margin_rows, 'pw', axis=0, tiled=True)  86.2 us
    all_gather x1, waiting for transfers between devices, shards(): span_whole = lax.all_gather(own_span, 'pw', axis=0, tiled=True)  76.6 us
    ppermute x2, waiting for transfers between devices, from_behind(): return lax.ppermute(block, axis, route)  46.6 us
    ppermute x7, waiting for transfers between devices, shifted(): return lax.ppermute(shard, axis, pairs)  38.3 us
    slice x8, local copies, waits for them, and re-layouts, complex_rows(): right_re = right[:, 0]  14.8 us
  transfers between devices with their start and end apart: 12, of which 12 were waited for; matrix products, arithmetic and copies ran while one was open for 0% of the time, Pallas kernels for 0%

commit v1 on v0

v1 whole, which is shorter than its diff:
```python
import functools
import heapq

import jax
import jax.numpy as jnp
from jax import lax
from jax.experimental import pallas as pl
from jax.experimental.pallas import tpu as pltpu
from jax.sharding import PartitionSpec as P

F32 = jnp.float32
BF16 = jnp.bfloat16
WIDTH = 128
SEMS = 256


def high_low(value):
    high = value.astype(BF16)
    return high, (value - high.astype(F32)).astype(BF16)


def dot(left, right):
    return jnp.dot(left, right, preferred_element_type=F32)


def dot_t(left, right):
    return lax.dot_general(left, right, (((1,), (1,)), ((), ())), preferred_element_type=F32)


def kernel(
    ka_size, zsize,
    re_hbm, im_hbm, out_ref,
    st_re, st_im, halo_re, halo_im, part, core_in, plus_in, minus_in, y_in, full,
    lhs0, m0_high, m0_low, p_high, p_low, rows_in, rows_out, stack,
    load_sem, send_sem, recv_sem,
):
    bands = st_re.shape[1]
    chunks = bands // WIDTH
    wide = 2 * WIDTH
    half = bands // 2
    piece = half // zsize
    small = piece // 2
    reach = zsize // 2
    own = rows_in.shape[0]

    ka = lax.axis_index("ka")
    pw = lax.axis_index("pw")
    core = lax.rem(pw, 2)
    z = lax.rem(pw // 2, zsize)
    yhi = pw // (2 * zsize)

    def pw_of(y, zz, c):
        return (y * zsize + zz) * 2 + c

    def up(n):
        return lax.rem(z + n, zsize)

    def down(n):
        return lax.rem(z + zsize - n, zsize)

    to_core = {"ka": ka, "pw": pw_of(yhi, z, 1 - core)}
    to_up = {"ka": ka, "pw": pw_of(yhi, up(1), core)}
    to_down = {"ka": ka, "pw": pw_of(yhi, down(1), core)}
    to_y = {"ka": ka, "pw": pw_of(1 - yhi, z, core)}
    to_next = {"ka": lax.rem(ka + 1, ka_size), "pw": pw}
    to_prev = {"ka": lax.rem(ka + ka_size - 1, ka_size), "pw": pw}

    loads = [
        pltpu.make_async_copy(re_hbm, st_re, load_sem.at[0]),
        pltpu.make_async_copy(im_hbm, st_im, load_sem.at[1]),
    ]
    for load in loads:
        load.start()

    barrier = pltpu.get_barrier_semaphore()
    partners = (to_core, to_up, to_down, to_y, to_next, to_prev)
    for partner in partners:
        pl.semaphore_signal(barrier, inc=1, device_id=partner, device_id_type=pl.DeviceIdType.MESH)
    pl.semaphore_wait(barrier, len(partners))

    started = []

    def copy(src, dst, device, start=True):
        n = len(started)
        made = pltpu.make_async_remote_copy(
            src_ref=src, dst_ref=dst, send_sem=send_sem.at[n], recv_sem=recv_sem.at[n],
            device_id=device, device_id_type=pl.DeviceIdType.MESH,
        )
        started.append(made)
        if start:
            made.start()
        return made

    halo = []
    for chunk in range(chunks):
        rows = pl.ds(chunk * WIDTH, WIDTH)
        halo.append((
            copy(re_hbm.at[0, rows], halo_re.at[rows], to_prev),
            copy(im_hbm.at[0, rows], halo_im.at[rows], to_prev),
        ))
    for load in loads:
        load.wait()

    def rows_of(zz, c, offset=0, count=None):
        count = piece if count is None else count
        start = c * half + zz * piece + offset
        return pl.ds(pl.multiple_of(start, small), count)

    def partial_sum(k, chunk, slot):
        columns = pl.ds(chunk * WIDTH, WIDTH)
        if k == 0:
            right_re, right_im = st_re[1, columns], st_im[1, columns]
        else:
            right_re, right_im = halo_re[columns], halo_im[columns]
        tile = min(bands, 256)

        @pl.loop(0, bands // tile)
        def _(step):
            rows = pl.ds(pl.multiple_of(step * tile, tile), tile)
            left_re, left_im = st_re[k, rows], st_im[k, rows]
            part[slot, rows, :WIDTH] = dot_t(left_re, right_re) + dot_t(left_im, right_im)
            part[slot, rows, WIDTH:] = dot_t(left_re, right_im) - dot_t(left_im, right_re)

    def finish_first(chunk, slot):
        columns = pl.ds(chunk * WIDTH, WIDTH)
        both = pl.ds(chunk * wide, wide)
        high, low = high_low(full[slot])
        m0_high[:, both] = high
        m0_low[:, both] = low
        lhs0[0, :, columns] = high[:, :WIDTH]
        lhs0[1, :, columns] = low[:, :WIDTH]
        lhs0[2, :, columns] = high[:, WIDTH:]
        lhs0[3, :, columns] = low[:, WIDTH:]

    def finish_second(chunk, slot):
        both = pl.ds(chunk * wide, wide)
        high, low = high_low(full[slot])
        tile = min(bands, 128)

        @pl.loop(0, bands // tile)
        def _(step):
            rows = pl.ds(pl.multiple_of(step * tile, tile), tile)
            re_high, re_low = lhs0[0, rows], lhs0[1, rows]
            im_high, im_low = lhs0[2, rows], lhs0[3, rows]
            by_re = dot(re_high, high) + (dot(re_low, high) + dot(re_high, low))
            by_im = dot(im_high, high) + (dot(im_low, high) + dot(im_high, low))
            new_re = by_re[:, :WIDTH] - by_im[:, WIDTH:]
            new_im = by_re[:, WIDTH:] + by_im[:, :WIDTH]
            span_high, span_low = high_low(jnp.concatenate([new_re, new_im], 1))
            p_high[rows, both] = span_high
            p_low[rows, both] = span_low

    def margin_chunk(k, chunk):
        slot = k * chunks + chunk
        if k == 1:
            halo[chunk][0].wait_recv()
            halo[chunk][1].wait_recv()
        partial_sum(k, chunk, slot)
        mine = pl.ds(pl.multiple_of(core * half, half), half)
        theirs = pl.ds(pl.multiple_of((1 - core) * half, half), half)
        crossing = copy(part.at[slot, theirs], core_in.at[slot], to_core)
        yield 1.6
        crossing.wait_recv()
        part[slot, mine] = part[slot, mine] + core_in[slot]
        far = up(reach)
        going_up = copy(
            part.at[slot, rows_of(far, core, 0, small)], plus_in.at[slot, 0, pl.ds(0, small)], to_up
        )
        going_down = copy(
            part.at[slot, rows_of(far, core, small, small)], minus_in.at[slot, 0, pl.ds(small, small)], to_down
        )
        yield 2.2
        for step in range(1, reach):
            going_up.wait_recv()
            going_down.wait_recv()
            there_up, there_down = up(reach - step), down(reach - step)
            if step == 1:
                at_up, at_down = rows_of(there_up, core, 0, small), rows_of(there_down, core, small, small)
                got_up, got_down = plus_in[slot, 0, :small], minus_in[slot, 0, small:]
            else:
                at_up, at_down = rows_of(there_up, core), rows_of(there_down, core)
                got_up, got_down = plus_in[slot, step - 1], minus_in[slot, step - 1]
            part[slot, at_up] = part[slot, at_up] + got_up
            part[slot, at_down] = part[slot, at_down] + got_down
            going_up = copy(part.at[slot, rows_of(there_up, core)], plus_in.at[slot, step], to_up)
            going_down = copy(part.at[slot, rows_of(there_down, core)], minus_in.at[slot, step], to_down)
            yield 2.5
        going_up.wait_recv()
        going_down.wait_recv()
        here = rows_of(z, core)
        if reach == 1:
            low_rows, high_rows = rows_of(z, core, 0, small), rows_of(z, core, small, small)
            part[slot, low_rows] = part[slot, low_rows] + plus_in[slot, 0, :small]
            part[slot, high_rows] = part[slot, high_rows] + minus_in[slot, 0, small:]
        else:
            part[slot, here] = part[slot, here] + plus_in[slot, reach - 1] + minus_in[slot, reach - 1]
        crossing = copy(part.at[slot, here], y_in.at[slot], to_y)
        yield 3.0
        crossing.wait_recv()
        full[slot, here] = part[slot, here] + y_in[slot]
        from_core = []

        def across(zz, offset=0, count=None):
            mine = full.at[slot, rows_of(zz, core, offset, count)]
            from_core.append(copy(mine, mine, to_core))

        def along(zz, device, offset=0, count=None):
            mine = full.at[slot, rows_of(zz, core, offset, count)]
            return copy(mine, mine, device)

        for step in range(reach):
            if step:
                going_up.wait_recv()
                going_down.wait_recv()
            last = step == reach - 1
            if last:
                going_up = along(down(step), to_up, 0, small)
                going_down = along(up(step), to_down, small, small)
            else:
                going_up = along(down(step), to_up)
                going_down = along(up(step), to_down)
            across(down(step))
            if step:
                across(up(step))
            yield 2.5
        going_up.wait_recv()
        going_down.wait_recv()
        across(down(reach))
        yield 1.2
        for crossing in from_core:
            crossing.wait_recv()
        if k == 0:
            finish_first(chunk, slot)
        else:
            finish_second(chunk, slot)

    order = []
    for chunk in range(chunks):
        order.append((1.0 + 0.7 * chunk, len(order), margin_chunk(0, chunk)))
    for chunk in range(chunks):
        order.append((11.5 * (chunk + 1), len(order), margin_chunk(1, chunk)))
    heapq.heapify(order)
    while order:
        when, n, steps = heapq.heappop(order)
        wait = next(steps, None)
        if wait is not None:
            heapq.heappush(order, (when + wait, n, steps))

    def apply(high_ref, low_ref):
        left = stack[...]
        short = jnp.concatenate([left[:own], left[2 * own:3 * own]], 0)
        pieces_re, pieces_im = [], []
        for chunk in range(chunks):
            both = pl.ds(chunk * wide, wide)
            with_high = dot(left, high_ref[:, both])
            with_low = dot(short, low_ref[:, both])
            by_re = with_high[:own] + (with_high[own:2 * own] + with_low[:own])
            by_im = with_high[2 * own:3 * own] + (with_high[3 * own:] + with_low[own:])
            pieces_re.append(by_re[:, :WIDTH] - by_im[:, WIDTH:])
            pieces_im.append(by_re[:, WIDTH:] + by_im[:, :WIDTH])
        return jnp.concatenate(pieces_re, 1), jnp.concatenate(pieces_im, 1)

    handed = copy(rows_out, rows_in, to_next, start=False)

    @pl.when(ka == 0)
    def _():
        row = lax.broadcasted_iota(jnp.int32, (own, 2 * bands), 0) + pw * own
        column = lax.broadcasted_iota(jnp.int32, (own, 2 * bands), 1)
        one = (row == column).astype(F32)
        high, low = high_low(one)
        stack[...] = jnp.concatenate([high[:, :bands], low[:, :bands], high[:, bands:], low[:, bands:]], 0)

    @pl.when(ka > 0)
    def _():
        handed.wait_recv()
        high, low = high_low(rows_in[...])
        stack[...] = jnp.concatenate([high[:, :bands], low[:, :bands], high[:, bands:], low[:, bands:]], 0)

    line_re, line_im = apply(p_high, p_low)
    rows_out[:, :bands] = line_re
    rows_out[:, bands:] = line_im

    @pl.when(ka < ka_size - 1)
    def _():
        handed.start()

    out_ref[1, 0] = line_re
    out_ref[1, 1] = line_im
    line_re, line_im = apply(m0_high, m0_low)
    out_ref[0, 0] = line_re
    out_ref[0, 1] = line_im

    for made in started[:-1]:
        made.wait_send()

    @pl.when(ka < ka_size - 1)
    def _():
        handed.wait_send()


def shards(ka_size, pw_size, states_re, states_im):
    _, bands, waves = states_re.shape
    zsize = pw_size // 4
    own = bands // pw_size
    chunks = bands // WIDTH
    slots = 2 * chunks
    wide = 2 * WIDTH
    half = bands // 2
    piece = half // zsize
    reach = zsize // 2
    any_space = pl.BlockSpec(memory_space=pl.ANY)
    lines = pl.pallas_call(
        functools.partial(kernel, ka_size, zsize),
        out_shape=jax.ShapeDtypeStruct((2, 2, own, bands), F32),
        in_specs=[any_space, any_space],
        out_specs=pl.BlockSpec(memory_space=pltpu.VMEM),
        scratch_shapes=[
            pltpu.VMEM((2, bands, waves), BF16),
            pltpu.VMEM((2, bands, waves), BF16),
            pltpu.VMEM((bands, waves), BF16),
            pltpu.VMEM((bands, waves), BF16),
            pltpu.VMEM((slots, bands, wide), F32),
            pltpu.VMEM((slots, half, wide), F32),
            pltpu.VMEM((slots, reach, piece, wide), F32),
            pltpu.VMEM((slots, reach, piece, wide), F32),
            pltpu.VMEM((slots, piece, wide), F32),
            pltpu.VMEM((slots, bands, wide), F32),
            pltpu.VMEM((4, bands, bands), BF16),
            pltpu.VMEM((bands, 2 * bands), BF16),
            pltpu.VMEM((bands, 2 * bands), BF16),
            pltpu.VMEM((bands, 2 * bands), BF16),
            pltpu.VMEM((bands, 2 * bands), BF16),
            pltpu.VMEM((own, 2 * bands), F32),
            pltpu.VMEM((own, 2 * bands), F32),
            pltpu.VMEM((4 * own, bands), BF16),
            pltpu.SemaphoreType.DMA((2,)),
            pltpu.SemaphoreType.DMA((SEMS,)),
            pltpu.SemaphoreType.DMA((SEMS,)),
        ],
        compiler_params=pltpu.CompilerParams(
            collective_id=0, has_side_effects=True, vmem_limit_bytes=56 * 1024 * 1024
        ),
    )(states_re, states_im)
    return jnp.transpose(lines, (0, 2, 1, 3))


def solution(mesh):
    in_specs = (P("ka", None, "pw"), P("ka", None, "pw"))
    out_specs = P("ka", "pw", None, None)
    body = functools.partial(shards, mesh.shape["ka"], mesh.shape["pw"])
    return jax.shard_map(body, mesh=mesh, in_specs=in_specs, out_specs=out_specs, check_vma=False)
```

time: 636 us -> 160 us (0.25); the launches traced: 625 us -> 160 us
  waiting for transfers between devices: 527 us -> 0 us
  Pallas kernels: 0 us -> 159 us
  matrix products: 34.8 us -> 0 us
  local copies, waits for them, and re-layouts: 34.6 us -> 1.66 us
  between operations: 13.9 us -> 0.01 us
  starting transfers between devices: 10.6 us -> 0 us
    unnamed x4 -> x0, waiting for transfers between devices: 280 us -> none
    all_gather x2 -> x0, waiting for transfers between devices: 163 us -> none  [the longest x1 86.2 us: shards(): margin_full = lax.all_gather(margin_rows, 'pw', axis=0, tiled=True)]
    pallas_call x0 -> x1, Pallas kernels: none -> 159 us  [shards(): pl.pallas_call(functools.partial(kernel, ka_size, zsize), out_shape=jax.S...]
    ppermute x9 -> x0, waiting for transfers between devices: 84.9 us -> none  [the longest x2 46.6 us: from_behind(): return lax.ppermute(block, axis, route)]
    dot_general x48 -> x0, matrix products: 34.8 us -> none  [the longest x11 8.03 us: complex_rows(): jnp.dot(left_re, right_im, precision=highest, preferred_element_type=jnp....]
    slice x10 -> x0, local copies, waits for them, and re-layouts: 16.8 us -> none  [the longest x8 14.8 us: complex_rows(): right_re = right[:, 0]]
    ppermute x9 -> x0, starting transfers between devices: 10.6 us -> none  [the longest x7 9.04 us: shifted(): return lax.ppermute(shard, axis, pairs)]
    another operation x2 -> x0, local copies, waits for them, and re-layouts: 8.09 us -> none  [the longest x1 7.34 us: shards(): jnp.stack([real_part, imag_part], 2)]
  transfers between devices with their start and end apart: 12 -> 0, of which waited for: 12 -> 0; matrix products, arithmetic and copies ran while one was open for 0% -> 0% of each run, Pallas kernels for 0% -> 0%
where the time goes in v1:
time: 160 us
  Pallas kernels  159 us (99%)
  local copies, waits for them, and re-layouts  1.66 us (1%)
    pallas_call x1, Pallas kernels, shards(): pl.pallas_call(functools.partial(kernel, ka_size, zsize), out_shape=jax.S...  159 us

profile of v1, /device:TPU:14, one launch (start us, length us, event | category | flops | bytes accessed | tf_op | source)
XLA Modules:
  0.0 160.3 jit_solution(8048588718612670629)
XLA Ops:
  0.0 158.7 %shard_map.28 = f32[2,2,16,512]{3,2,1,0:T(8,128)} custom-call(bf16[2,512,1024]{2,1,0:T(8,128)(2,1)} %re_hbm.1, bf16[2,512,1024]{2,1,0:T(8,128)(2,1)} %im_hbm.1), custom_call_target="tpu_custom_call" | custom-call | tf_op jit(solution)/shard_map/pallas_call | solution.py:312
  158.7 1.7 %copy.3 = f32[2,16,2,512]{3,2,1,0:T(2,128)} copy(f32[2,16,2,512]{3,1,2,0:T(8,128)} %bitcast.1) | data formatting | bytes 262144 | tf_op jit(solution)/shard_map/transpose | solution.py:344

commit v2 on v1

v2 whole, which is shorter than its diff:
```python
import functools
import heapq

import jax
import jax.numpy as jnp
from jax import lax
from jax.experimental import pallas as pl
from jax.experimental.pallas import tpu as pltpu
from jax.sharding import PartitionSpec as P

F32 = jnp.float32
BF16 = jnp.bfloat16
WIDTH = 128
SEMS = 256


def high_low(value):
    high = value.astype(BF16)
    return high, (value - high.astype(F32)).astype(BF16)


def dot(left, right):
    return jnp.dot(left, right, preferred_element_type=F32)


def dot_t(left, right):
    return lax.dot_general(left, right, (((1,), (1,)), ((), ())), preferred_element_type=F32)


def kernel(
    ka_size, zsize,
    re_hbm, im_hbm, out_ref,
    st_re, st_im, part, core_in, plus_in, minus_in, y_in, mix_in, full,
    lhs0, m0_high, m0_low, p_high, p_low, rows_in, rows_out, stack,
    load_sem, send_sem, recv_sem,
):
    bands = st_re.shape[1]
    chunks = bands // WIDTH
    wide = 2 * WIDTH
    half = bands // 2
    piece = half // zsize
    reach = zsize // 2
    own = rows_in.shape[0]

    ka = lax.axis_index("ka")
    pw = lax.axis_index("pw")
    core = lax.rem(pw, 2)
    z = lax.rem(pw // 2, zsize)
    yhi = pw // (2 * zsize)

    def device(k, y, zz, c):
        return {"ka": lax.rem(k + ka_size, ka_size), "pw": (y * zsize + zz) * 2 + c}

    def up(n):
        return lax.rem(z + n, zsize)

    def down(n):
        return lax.rem(z + zsize - n, zsize)

    to_core = device(ka, yhi, z, 1 - core)
    to_up = device(ka, yhi, up(1), core)
    to_down = device(ka, yhi, down(1), core)
    to_y = device(ka, 1 - yhi, z, core)
    to_next = device(ka + 1, yhi, z, core)
    to_prev = device(ka - 1, yhi, z, core)
    to_halo = device(ka - 1 + 2 * core, yhi, z, core)
    from_halo = device(ka + 1 - 2 * core, yhi, z, core)
    to_mix = (
        device(ka - core, yhi, z, 1 - core),
        device(ka - core, 1 - yhi, z, core),
        device(ka - core, 1 - yhi, z, 1 - core),
        to_prev,
    )
    from_mix = (
        device(ka + 1 - core, yhi, z, 1 - core),
        device(ka + core, 1 - yhi, z, core),
        device(ka + 1 - core, 1 - yhi, z, 1 - core),
        to_next,
    )

    loads = [
        pltpu.make_async_copy(re_hbm, st_re.at[pl.ds(0, 2)], load_sem.at[0]),
        pltpu.make_async_copy(im_hbm, st_im.at[pl.ds(0, 2)], load_sem.at[1]),
    ]
    for load in loads:
        load.start()

    barrier = pltpu.get_barrier_semaphore()
    senders = (to_core, to_up, to_down, to_y, to_prev, from_halo) + from_mix
    for sender in senders:
        pl.semaphore_signal(barrier, inc=1, device_id=sender, device_id_type=pl.DeviceIdType.MESH)
    pl.semaphore_wait(barrier, len(senders))

    started = []
    numbered = [0]

    def prepare(src, dst, target):
        n = numbered[0]
        numbered[0] += 1
        return pltpu.make_async_remote_copy(
            src_ref=src, dst_ref=dst, send_sem=send_sem.at[n], recv_sem=recv_sem.at[n],
            device_id=target, device_id_type=pl.DeviceIdType.MESH,
        )

    def copy(src, dst, target):
        made = prepare(src, dst, target)
        made.start()
        started.append(made)
        return made

    halo = (copy(re_hbm.at[core], st_re.at[2], to_halo), copy(im_hbm.at[core], st_im.at[2], to_halo))
    for load in loads:
        load.wait()

    def partial_sum(left, right, chunk, slot):
        columns = pl.ds(chunk * WIDTH, WIDTH)
        right_re, right_im = st_re[right, columns], st_im[right, columns]
        tile = min(bands, 256)

        @pl.loop(0, bands // tile)
        def _(step):
            rows = pl.ds(pl.multiple_of(step * tile, tile), tile)
            left_re, left_im = st_re[left, rows], st_im[left, rows]
            part[slot, rows, :WIDTH] = dot_t(left_re, right_re) + dot_t(left_im, right_im)
            part[slot, rows, WIDTH:] = dot_t(left_re, right_im) - dot_t(left_im, right_re)

    def finish_first(chunk, slot):
        columns = pl.ds(chunk * WIDTH, WIDTH)
        both = pl.ds(chunk * wide, wide)
        high, low = high_low(full[slot])
        m0_high[:, both] = high
        m0_low[:, both] = low
        lhs0[0, :, columns] = high[:, :WIDTH]
        lhs0[1, :, columns] = low[:, :WIDTH]
        lhs0[2, :, columns] = high[:, WIDTH:]
        lhs0[3, :, columns] = low[:, WIDTH:]

    def finish_second(chunk, slot):
        both = pl.ds(chunk * wide, wide)
        high, low = high_low(full[slot])
        tile = min(bands, 128)

        @pl.loop(0, bands // tile)
        def _(step):
            rows = pl.ds(pl.multiple_of(step * tile, tile), tile)
            re_high, re_low = lhs0[0, rows], lhs0[1, rows]
            im_high, im_low = lhs0[2, rows], lhs0[3, rows]
            by_re = dot(re_high, high) + (dot(re_low, high) + dot(re_high, low))
            by_im = dot(im_high, high) + (dot(im_low, high) + dot(im_high, low))
            new_re = by_re[:, :WIDTH] - by_im[:, WIDTH:]
            new_im = by_re[:, WIDTH:] + by_im[:, :WIDTH]
            span_high, span_low = high_low(jnp.concatenate([new_re, new_im], 1))
            p_high[rows, both] = span_high
            p_low[rows, both] = span_low

    def scatter(slot, base, size, pace):
        small = size // 2

        def rows(zz, offset=0, count=size):
            return pl.ds(pl.multiple_of(base + zz * size + offset, 8), count)

        far = up(reach)
        going_up = copy(
            part.at[slot, rows(far, 0, small)], plus_in.at[slot, 0, pl.ds(0, small)], to_up
        )
        going_down = copy(
            part.at[slot, rows(far, small, small)], minus_in.at[slot, 0, pl.ds(small, small)], to_down
        )
        yield pace
        for step in range(1, reach):
            going_up.wait_recv()
            going_down.wait_recv()
            there_up, there_down = up(reach - step), down(reach - step)
            if step == 1:
                at_up, at_down = rows(there_up, 0, small), rows(there_down, small, small)
                got_up, got_down = plus_in[slot, 0, :small], minus_in[slot, 0, small:size]
            else:
                at_up, at_down = rows(there_up), rows(there_down)
                got_up, got_down = plus_in[slot, step - 1, :size], minus_in[slot, step - 1, :size]
            part[slot, at_up] = part[slot, at_up] + got_up
            part[slot, at_down] = part[slot, at_down] + got_down
            going_up = copy(part.at[slot, rows(there_up)], plus_in.at[slot, step, pl.ds(0, size)], to_up)
            going_down = copy(part.at[slot, rows(there_down)], minus_in.at[slot, step, pl.ds(0, size)], to_down)
            yield pace
        going_up.wait_recv()
        going_down.wait_recv()
        if reach == 1:
            first, second = rows(z, 0, small), rows(z, small, small)
            part[slot, first] = part[slot, first] + plus_in[slot, 0, :small]
            part[slot, second] = part[slot, second] + minus_in[slot, 0, small:size]
        else:
            here = rows(z)
            part[slot, here] = part[slot, here] + plus_in[slot, reach - 1, :size] + minus_in[slot, reach - 1, :size]

    def gather(slot, base, stride, pace):
        small = piece // 2
        from_core = []

        def rows(zz, offset=0, count=piece):
            return pl.ds(pl.multiple_of(base + zz * stride + offset, 8), count)

        def send(target, zz, offset=0, count=piece):
            mine = full.at[slot, rows(zz, offset, count)]
            return copy(mine, mine, target)

        for step in range(reach):
            if step:
                going_up.wait_recv()
                going_down.wait_recv()
            if step == reach - 1:
                going_up = send(to_up, down(step), 0, small)
                going_down = send(to_down, up(step), small, small)
            else:
                going_up = send(to_up, down(step))
                going_down = send(to_down, up(step))
            from_core.append(send(to_core, down(step)))
            if step:
                from_core.append(send(to_core, up(step)))
            yield pace
        going_up.wait_recv()
        going_down.wait_recv()
        from_core.append(send(to_core, down(reach)))
        yield 1.2
        for crossing in from_core:
            crossing.wait_recv()

    def first_margin(chunk):
        slot = chunk
        partial_sum(0, 1, chunk, slot)
        mine = pl.ds(pl.multiple_of(core * half, half), half)
        theirs = pl.ds(pl.multiple_of((1 - core) * half, half), half)
        crossing = copy(part.at[slot, theirs], core_in.at[chunk], to_core)
        yield 2.5
        crossing.wait_recv()
        part[slot, mine] = part[slot, mine] + core_in[chunk]
        yield from scatter(slot, core * half, piece, 3.2)
        here = pl.ds(pl.multiple_of(core * half + z * piece, 8), piece)
        crossing = copy(part.at[slot, here], y_in.at[chunk], to_y)
        yield 4.0
        crossing.wait_recv()
        full[slot, here] = part[slot, here] + y_in[chunk]
        yield from gather(slot, core * half, piece, 3.6)
        finish_first(chunk, slot)

    conditional = []

    def second_margin(chunk):
        slot = chunks + chunk
        if chunk == 0:
            for arriving in halo:
                arriving.wait_recv()
        partial_sum(1 + core, 2 - 2 * core, chunk, slot)
        yield from scatter(slot, 0, 2 * piece, 5.0)

        def here(c):
            return pl.ds(pl.multiple_of(z * 2 * piece + c * piece, 8), piece)

        arriving = [
            copy(part.at[slot, here(1 - core)], mix_in.at[chunk, 0], to_mix[0]),
            copy(part.at[slot, here(core)], mix_in.at[chunk, 1], to_mix[1]),
            copy(part.at[slot, here(1 - core)], mix_in.at[chunk, 2], to_mix[2]),
        ]
        last = prepare(part.at[slot, here(core)], mix_in.at[chunk, 3], to_mix[3])
        conditional.append(last)

        @pl.when(core == 1)
        def _():
            last.start()

        @pl.when(core == 0)
        def _():
            mix_in[chunk, 3] = part[slot, here(core)]

        yield 4.5
        for crossing in arriving:
            crossing.wait_recv()

        @pl.when(core == 1)
        def _():
            last.wait_recv()

        full[slot, here(core)] = (mix_in[chunk, 0] + mix_in[chunk, 1]) + (mix_in[chunk, 2] + mix_in[chunk, 3])
        yield from gather(slot, core * piece, 2 * piece, 3.6)
        finish_second(chunk, slot)

    order = []
    for chunk in range(chunks):
        order.append((2.0 + 0.8 * chunk, len(order), first_margin(chunk)))
    for chunk in range(chunks):
        order.append((25.0 + 0.8 * chunk, len(order), second_margin(chunk)))
    heapq.heapify(order)
    while order:
        when, n, steps = heapq.heappop(order)
        wait = next(steps, None)
        if wait is not None:
            heapq.heappush(order, (when + wait, n, steps))

    def apply(high_ref, low_ref):
        left = stack[...]
        short = jnp.concatenate([left[:own], left[2 * own:3 * own]], 0)
        pieces_re, pieces_im = [], []
        for chunk in range(chunks):
            both = pl.ds(chunk * wide, wide)
            with_high = dot(left, high_ref[:, both])
            with_low = dot(short, low_ref[:, both])
            by_re = with_high[:own] + (with_high[own:2 * own] + with_low[:own])
            by_im = with_high[2 * own:3 * own] + (with_high[3 * own:] + with_low[own:])
            pieces_re.append(by_re[:, :WIDTH] - by_im[:, WIDTH:])
            pieces_im.append(by_re[:, WIDTH:] + by_im[:, :WIDTH])
        return jnp.concatenate(pieces_re, 1), jnp.concatenate(pieces_im, 1)

    handed = prepare(rows_out, rows_in, to_next)

    @pl.when(ka == 0)
    def _():
        row = lax.broadcasted_iota(jnp.int32, (own, 2 * bands), 0) + pw * own
        column = lax.broadcasted_iota(jnp.int32, (own, 2 * bands), 1)
        one = (row == column).astype(F32)
        high, low = high_low(one)
        stack[...] = jnp.concatenate([high[:, :bands], low[:, :bands], high[:, bands:], low[:, bands:]], 0)

    @pl.when(ka > 0)
    def _():
        handed.wait_recv()
        high, low = high_low(rows_in[...])
        stack[...] = jnp.concatenate([high[:, :bands], low[:, :bands], high[:, bands:], low[:, bands:]], 0)

    line_re, line_im = apply(p_high, p_low)
    rows_out[:, :bands] = line_re
    rows_out[:, bands:] = line_im

    @pl.when(ka < ka_size - 1)
    def _():
        handed.start()

    out_ref[1, 0] = line_re
    out_ref[1, 1] = line_im
    line_re, line_im = apply(m0_high, m0_low)
    out_ref[0, 0] = line_re
    out_ref[0, 1] = line_im

    for made in started:
        made.wait_send()

    @pl.when(core == 1)
    def _():
        for made in conditional:
            made.wait_send()

    @pl.when(ka < ka_size - 1)
    def _():
        handed.wait_send()


def shards(ka_size, pw_size, states_re, states_im):
    _, bands, waves = states_re.shape
    zsize = pw_size // 4
    own = bands // pw_size
    chunks = bands // WIDTH
    slots = 2 * chunks
    wide = 2 * WIDTH
    half = bands // 2
    piece = half // zsize
    reach = zsize // 2
    any_space = pl.BlockSpec(memory_space=pl.ANY)
    lines = pl.pallas_call(
        functools.partial(kernel, ka_size, zsize),
        out_shape=jax.ShapeDtypeStruct((2, 2, own, bands), F32),
        in_specs=[any_space, any_space],
        out_specs=pl.BlockSpec(memory_space=pltpu.VMEM),
        scratch_shapes=[
            pltpu.VMEM((3, bands, waves), BF16),
            pltpu.VMEM((3, bands, waves), BF16),
            pltpu.VMEM((slots, bands, wide), F32),
            pltpu.VMEM((chunks, half, wide), F32),
            pltpu.VMEM((slots, reach, 2 * piece, wide), F32),
            pltpu.VMEM((slots, reach, 2 * piece, wide), F32),
            pltpu.VMEM((chunks, piece, wide), F32),
            pltpu.VMEM((chunks, 4, piece, wide), F32),
            pltpu.VMEM((slots, bands, wide), F32),
            pltpu.VMEM((4, bands, bands), BF16),
            pltpu.VMEM((bands, 2 * bands), BF16),
            pltpu.VMEM((bands, 2 * bands), BF16),
            pltpu.VMEM((bands, 2 * bands), BF16),
            pltpu.VMEM((bands, 2 * bands), BF16),
            pltpu.VMEM((own, 2 * bands), F32),
            pltpu.VMEM((own, 2 * bands), F32),
            pltpu.VMEM((4 * own, bands), BF16),
            pltpu.SemaphoreType.DMA((2,)),
            pltpu.SemaphoreType.DMA((SEMS,)),
            pltpu.SemaphoreType.DMA((SEMS,)),
        ],
        compiler_params=pltpu.CompilerParams(
            collective_id=0, has_side_effects=True, vmem_limit_bytes=56 * 1024 * 1024
        ),
    )(states_re, states_im)
    return jnp.transpose(lines, (0, 2, 1, 3))


def solution(mesh):
    in_specs = (P("ka", None, "pw"), P("ka", None, "pw"))
    out_specs = P("ka", "pw", None, None)
    body = functools.partial(shards, mesh.shape["ka"], mesh.shape["pw"])
    return jax.shard_map(body, mesh=mesh, in_specs=in_specs, out_specs=out_specs, check_vma=False)
```

time: 160 us -> 126 us (0.79)
  Pallas kernels: 159 us -> 124 us
    pallas_call x1, Pallas kernels: 159 us -> 124 us  [shards(): pl.pallas_call(functools.partial(kernel, ka_size, zsize), out_shape=jax.S...]
where the time goes in v2:
time: 126 us
  Pallas kernels  124 us (98%)
  local copies, waits for them, and re-layouts  1.66 us (1%)
    pallas_call x1, Pallas kernels, shards(): pl.pallas_call(functools.partial(kernel, ka_size, zsize), out_shape=jax.S...  124 us

profile of v2, /device:TPU:14, one launch (start us, length us, event | category | flops | bytes accessed | tf_op | source)
XLA Modules:
  0.0 126.0 jit_solution(12581721385082253613)
XLA Ops:
  0.0 124.4 %shard_map.28 = f32[2,2,16,512]{3,2,1,0:T(8,128)} custom-call(bf16[2,512,1024]{2,1,0:T(8,128)(2,1)} %re_hbm.1, bf16[2,512,1024]{2,1,0:T(8,128)(2,1)} %im_hbm.1), custom_call_target="tpu_custom_call" | custom-call | tf_op jit(solution)/shard_map/pallas_call | solution.py:366
  124.4 1.7 %copy.3 = f32[2,16,2,512]{3,2,1,0:T(2,128)} copy(f32[2,16,2,512]{3,1,2,0:T(8,128)} %bitcast.1) | data formatting | bytes 262144 | tf_op jit(solution)/shard_map/transpose | solution.py:397

commit v3 on v2

v3 whole, which is shorter than its diff:
```python
import functools
import heapq

import jax
import jax.numpy as jnp
from jax import lax
from jax.experimental import pallas as pl
from jax.experimental.pallas import tpu as pltpu
from jax.sharding import PartitionSpec as P

F32 = jnp.float32
BF16 = jnp.bfloat16
WIDTH = 128
SEMS = 256
DEPTH = 2
FIRST_START = 2.0
FIRST_PACE = 1.5
GATHER_START = 32.0
SPREAD_PACE = 1.5
IN_TWO = (0, 1, 2, 3)
FINAL_PACE = 4.0
SUM_PACE = 4.2
HALO_START = 8.0
HALO_PACE = 5.8


def high_low(value):
    high = value.astype(BF16)
    return high, (value - high.astype(F32)).astype(BF16)


def dot(left, right):
    return jnp.dot(left, right, preferred_element_type=F32)


def dot_t(left, right):
    return lax.dot_general(left, right, (((1,), (1,)), ((), ())), preferred_element_type=F32)


def kernel(
    ka_size, zsize,
    re_hbm, im_hbm, out_ref,
    st, part0, part1, core_in, plus0, minus0, plus1, minus1, y_in, mix_columns, mix_rows, full0, full1,
    lhs0, m0_high, m0_low, p_high, p_low, rows_in, rows_out, stack,
    load_sem, send_sem, recv_sem,
):
    chunks, waves = st.shape[1], st.shape[4]
    bands = chunks * WIDTH
    wide = 2 * WIDTH
    half = bands // 2
    piece = half // zsize
    strip = WIDTH // zsize
    thin = strip // 2
    reach = zsize // 2
    own = rows_in.shape[0]

    ka = lax.axis_index("ka")
    pw = lax.axis_index("pw")
    core = lax.rem(pw, 2)
    z = lax.rem(pw // 2, zsize)
    yhi = pw // (2 * zsize)

    def device(k, y, zz, c):
        return {"ka": lax.rem(k + ka_size, ka_size), "pw": (y * zsize + zz) * 2 + c}

    def up(n):
        return lax.rem(z + n, zsize)

    def down(n):
        return lax.rem(z + zsize - n, zsize)

    to_core = device(ka, yhi, z, 1 - core)
    to_up = device(ka, yhi, up(1), core)
    to_down = device(ka, yhi, down(1), core)
    to_up2 = device(ka, yhi, up(2), core)
    to_down2 = device(ka, yhi, down(2), core)
    to_y = device(ka, 1 - yhi, z, core)
    to_next = device(ka + 1, yhi, z, core)
    to_prev = device(ka - 1, yhi, z, core)
    to_halo = device(ka - 1 + 2 * core, yhi, z, core)
    from_halo = device(ka + 1 - 2 * core, yhi, z, core)
    to_mix = (
        device(ka - core, yhi, z, 1 - core),
        device(ka - core, 1 - yhi, z, core),
        device(ka - core, 1 - yhi, z, 1 - core),
        to_prev,
    )
    from_mix = (
        device(ka + 1 - core, yhi, z, 1 - core),
        device(ka + core, 1 - yhi, z, core),
        device(ka + 1 - core, 1 - yhi, z, 1 - core),
        to_next,
    )

    loads = []
    for block in range(chunks):
        rows = pl.ds(block * WIDTH, WIDTH)
        for k in range(2):
            for n, hbm in enumerate((re_hbm, im_hbm)):
                loads.append(pltpu.make_async_copy(hbm.at[k, rows], st.at[k, block, n], load_sem.at[len(loads)]))
    for load in loads:
        load.start()

    barrier = pltpu.get_barrier_semaphore()
    senders = (to_core, to_up, to_down, to_y, to_prev, from_halo) + from_mix
    if reach == 4:
        senders += (to_up2, to_down2)
    for sender in senders:
        pl.semaphore_signal(barrier, inc=1, device_id=sender, device_id_type=pl.DeviceIdType.MESH)
    pl.semaphore_wait(barrier, len(senders))

    started = []
    numbered = [0]

    def prepare(src, dst, target, number=None):
        if number is None:
            number = numbered[0]
            numbered[0] += 1
        return pltpu.make_async_remote_copy(
            src_ref=src, dst_ref=dst, send_sem=send_sem.at[number], recv_sem=recv_sem.at[number],
            device_id=target, device_id_type=pl.DeviceIdType.MESH,
        )

    def copy(src, dst, target):
        made = prepare(src, dst, target)
        made.start()
        started.append(made)
        return made

    halo = []

    def states_across():
        for block in range(chunks):
            if block >= DEPTH:
                for made in halo[block - DEPTH]:
                    made.wait_send()
            rows = pl.ds(block * WIDTH, WIDTH)
            pair = [
                prepare(hbm.at[core, rows], st.at[2, block, n], to_halo) for n, hbm in enumerate((re_hbm, im_hbm))
            ]
            for made in pair:
                made.start()
            halo.append(pair)
            if block + 1 >= DEPTH:
                yield HALO_PACE
        for block in range(max(chunks - DEPTH, 0), chunks):
            for made in halo[block]:
                made.wait_send()

    def block_sum(left, right):
        both = dot_t(left.reshape(wide, waves), right.reshape(wide, waves))
        real = both[:WIDTH, :WIDTH] + both[WIDTH:, WIDTH:]
        imag = both[:WIDTH, WIDTH:] - both[WIDTH:, :WIDTH]
        return real, imag

    def finish_first(chunk):
        columns = pl.ds(chunk * WIDTH, WIDTH)
        both = pl.ds(chunk * wide, wide)
        high, low = high_low(full0[chunk])
        m0_high[:, both] = high
        m0_low[:, both] = low
        lhs0[0, :, columns] = high[:, :WIDTH]
        lhs0[1, :, columns] = low[:, :WIDTH]
        lhs0[2, :, columns] = high[:, WIDTH:]
        lhs0[3, :, columns] = low[:, WIDTH:]

    def finish_second(chunk):
        both = pl.ds(chunk * wide, wide)
        high, low = high_low(full1[chunk].reshape(bands, wide))

        @pl.loop(0, chunks)
        def _(step):
            rows = pl.ds(pl.multiple_of(step * WIDTH, WIDTH), WIDTH)
            re_high, re_low = lhs0[0, rows], lhs0[1, rows]
            im_high, im_low = lhs0[2, rows], lhs0[3, rows]
            by_re = dot(re_high, high) + (dot(re_low, high) + dot(re_high, low))
            by_im = dot(im_high, high) + (dot(im_low, high) + dot(im_high, low))
            new_re = by_re[:, :WIDTH] - by_im[:, WIDTH:]
            new_im = by_re[:, WIDTH:] + by_im[:, :WIDTH]
            span_high, span_low = high_low(jnp.concatenate([new_re, new_im], 1))
            p_high[rows, both] = span_high
            p_low[rows, both] = span_low

    def scatter(part, at, plus, minus, arrived, pace):
        def add(where, buffer, which):
            part[where] = part[where] + buffer[which]

        far = up(reach)
        going_up = copy(part.at[at(far, 0)], plus.at[arrived(0, 0)], to_up)
        going_down = copy(part.at[at(far, 1)], minus.at[arrived(0, 1)], to_down)
        yield pace
        for step in range(1, reach):
            going_up.wait_recv()
            going_down.wait_recv()
            there_up, there_down = up(reach - step), down(reach - step)
            if step == 1:
                add(at(there_up, 0), plus, arrived(0, 0))
                add(at(there_down, 1), minus, arrived(0, 1))
            else:
                add(at(there_up), plus, arrived(step - 1))
                add(at(there_down), minus, arrived(step - 1))
            going_up = copy(part.at[at(there_up)], plus.at[arrived(step)], to_up)
            going_down = copy(part.at[at(there_down)], minus.at[arrived(step)], to_down)
            yield pace
        going_up.wait_recv()
        going_down.wait_recv()
        if reach == 1:
            add(at(z, 0), plus, arrived(0, 0))
            add(at(z, 1), minus, arrived(0, 1))
        else:
            here = at(z)
            part[here] = part[here] + plus[arrived(reach - 1)] + minus[arrived(reach - 1)]

    def gather(full, at, pace):
        from_core = []

        def send(target, *which):
            mine = full.at[at(*which)]
            return copy(mine, mine, target)

        for step in range(reach):
            if step:
                going_up.wait_recv()
                going_down.wait_recv()
            if step == reach - 1:
                going_up = send(to_up, down(step), 0)
                going_down = send(to_down, up(step), 1)
            else:
                going_up = send(to_up, down(step))
                going_down = send(to_down, up(step))
            from_core.append(send(to_core, down(step)))
            if step:
                from_core.append(send(to_core, up(step)))
            yield pace
        going_up.wait_recv()
        going_down.wait_recv()
        from_core.append(send(to_core, down(reach)))
        yield 1.2
        for crossing in from_core:
            crossing.wait_recv()

    def gather_in_two(full, at, pace):
        def send(target, *which):
            mine = full.at[at(*which)]
            return copy(mine, mine, target)

        two_up, two_down = send(to_up2, z), send(to_down2, z)
        one_up, one_down = send(to_up, z), send(to_down, z)
        from_core = [send(to_core, z)]
        yield pace
        two_up.wait_recv()
        later = [send(to_up2, down(2), 0), send(to_up, down(2))]
        two_down.wait_recv()
        later += [send(to_down2, up(2), 1), send(to_down, up(2))]
        from_core += [send(to_core, down(2)), send(to_core, up(2))]
        one_up.wait_recv()
        one_down.wait_recv()
        from_core += [send(to_core, down(1)), send(to_core, up(1))]
        yield pace
        later[1].wait_recv()
        later[3].wait_recv()
        from_core += [send(to_core, down(3)), send(to_core, up(3))]
        later[0].wait_recv()
        later[2].wait_recv()
        from_core.append(send(to_core, up(4)))
        yield 2.0
        for crossing in from_core:
            crossing.wait_recv()

    def first_margin(chunk):
        if chunk == 0:
            for load in loads:
                load.wait()

        @pl.loop(0, chunks)
        def _(block):
            rows = pl.ds(pl.multiple_of(block * WIDTH, WIDTH), WIDTH)
            real, imag = block_sum(st[0, block], st[1, chunk])
            part0[chunk, rows, :WIDTH] = real
            part0[chunk, rows, WIDTH:] = imag

        mine = pl.ds(pl.multiple_of(core * half, half), half)
        theirs = pl.ds(pl.multiple_of((1 - core) * half, half), half)
        crossing = copy(part0.at[chunk, theirs], core_in.at[chunk], to_core)
        yield 2.5
        crossing.wait_recv()
        part0[chunk, mine] = part0[chunk, mine] + core_in[chunk]

        def at(zz, h=None):
            count = piece if h is None else piece // 2
            start = core * half + zz * piece + (h or 0) * count
            return chunk, pl.ds(pl.multiple_of(start, 8), count)

        def arrived(step, h=None):
            count = piece if h is None else piece // 2
            return chunk, step, pl.ds((h or 0) * count, count)

        yield from scatter(part0, at, plus0, minus0, arrived, 3.2)
        crossing = copy(part0.at[at(z)], y_in.at[chunk], to_y)
        yield GATHER_START - (FIRST_START + 15.3)
        crossing.wait_recv()
        full0[at(z)] = part0[at(z)] + y_in[chunk]
        yield from gather(full0, at, 3.6)
        finish_first(chunk)

    def blocks_of(h):
        return pl.ds(0, chunks) if h is None else pl.ds(h * (chunks // 2), chunks // 2)

    def second_margin(chunk):
        for arriving in halo[chunk]:
            arriving.wait_recv()

        @pl.loop(0, chunks)
        def _(block):
            left_block = block * (1 - core) + chunk * core
            right_block = block * core + chunk * (1 - core)
            real, imag = block_sum(st[1 + core, left_block], st[2 - 2 * core, right_block])
            part1[chunk, block, :, :WIDTH] = real
            part1[chunk, block, :, WIDTH:] = imag

        def at(zz, h=None):
            return chunk, blocks_of(h), pl.ds(pl.multiple_of(zz * strip, 8), strip)

        def arrived(step, h=None):
            return chunk, step, blocks_of(h)

        yield from scatter(part1, at, plus1, minus1, arrived, SUM_PACE)

        def rows(c):
            return chunk, slice(None), pl.ds(pl.multiple_of(z * strip + c * thin, 8), thin)

        number = numbered[0]
        numbered[0] += 4
        ways = ((1 - core, 0), (core, 1), (1 - core, 1), (core, 0))
        from_zero = [
            prepare(part1.at[rows(c)], mix_columns.at[chunk, far], to_mix[n], number + n)
            for n, (c, far) in enumerate(ways[:3])
        ]
        from_one = [
            prepare(part1.at[rows(c)], mix_rows.at[chunk, far], to_mix[n], number + n)
            for n, (c, far) in enumerate(ways)
        ]
        joined.extend(from_zero)
        conditional.append(from_one[3])

        @pl.when(core == 0)
        def _():
            for made in from_zero:
                made.start()
            mix_columns[chunk, 0] = part1[rows(core)]

        @pl.when(core == 1)
        def _():
            for made in from_one:
                made.start()

        yield 4.5
        for made in from_zero:
            made.wait_recv()

        @pl.when(core == 1)
        def _():
            from_one[3].wait_recv()

    conditional = []
    joined = []

    def spread(chunk):
        def at(zz, h=None):
            return chunk, blocks_of(h), pl.ds(pl.multiple_of(zz * strip + core * thin, 8), thin)

        full1[at(z)] = (mix_columns[chunk, 0] + mix_columns[chunk, 1]) + (mix_rows[:, 0, chunk] + mix_rows[:, 1, chunk])
        if reach == 4 and chunk in IN_TWO:
            yield from gather_in_two(full1, at, FINAL_PACE)
        else:
            yield from gather(full1, at, 3.6)
        assert firsts == chunks
        finish_second(chunk)

    order = [(0.0, 0, "halo", states_across())]
    for chunk in range(chunks):
        order.append((FIRST_START + FIRST_PACE * chunk, len(order), "first", first_margin(chunk)))
    for chunk in range(chunks):
        order.append((HALO_START + HALO_PACE * chunk, len(order), "second", second_margin(chunk)))
    heapq.heapify(order)
    firsts = seconds = 0
    while order:
        when, n, kind, steps = heapq.heappop(order)
        wait = next(steps, None)
        if wait is not None:
            heapq.heappush(order, (when + wait, n, kind, steps))
        firsts += wait is None and kind == "first"
        seconds += wait is None and kind == "second"
        if wait is None and kind == "second" and seconds == chunks:
            for chunk in range(chunks):
                heapq.heappush(order, (when + SPREAD_PACE * chunk, 100 + chunk, "spread", spread(chunk)))

    def apply(high_ref, low_ref):
        left = stack[...]
        short = jnp.concatenate([left[:own], left[2 * own:3 * own]], 0)
        pieces_re, pieces_im = [], []
        for chunk in range(chunks):
            both = pl.ds(chunk * wide, wide)
            with_high = dot(left, high_ref[:, both])
            with_low = dot(short, low_ref[:, both])
            by_re = with_high[:own] + (with_high[own:2 * own] + with_low[:own])
            by_im = with_high[2 * own:3 * own] + (with_high[3 * own:] + with_low[own:])
            pieces_re.append(by_re[:, :WIDTH] - by_im[:, WIDTH:])
            pieces_im.append(by_re[:, WIDTH:] + by_im[:, :WIDTH])
        return jnp.concatenate(pieces_re, 1), jnp.concatenate(pieces_im, 1)

    handed = prepare(rows_out, rows_in, to_next)

    @pl.when(ka == 0)
    def _():
        row = lax.broadcasted_iota(jnp.int32, (own, 2 * bands), 0) + pw * own
        column = lax.broadcasted_iota(jnp.int32, (own, 2 * bands), 1)
        one = (row == column).astype(F32)
        high, low = high_low(one)
        stack[...] = jnp.concatenate([high[:, :bands], low[:, :bands], high[:, bands:], low[:, bands:]], 0)

    @pl.when(ka > 0)
    def _():
        handed.wait_recv()
        high, low = high_low(rows_in[...])
        stack[...] = jnp.concatenate([high[:, :bands], low[:, :bands], high[:, bands:], low[:, bands:]], 0)

    line_re, line_im = apply(p_high, p_low)
    rows_out[:, :bands] = line_re
    rows_out[:, bands:] = line_im

    @pl.when(ka < ka_size - 1)
    def _():
        handed.start()

    out_ref[1, 0] = line_re
    out_ref[1, 1] = line_im
    line_re, line_im = apply(m0_high, m0_low)
    out_ref[0, 0] = line_re
    out_ref[0, 1] = line_im

    for made in started + joined:
        made.wait_send()

    @pl.when(core == 1)
    def _():
        for made in conditional:
            made.wait_send()

    @pl.when(ka < ka_size - 1)
    def _():
        handed.wait_send()


def shards(ka_size, pw_size, states_re, states_im):
    _, bands, waves = states_re.shape
    zsize = pw_size // 4
    own = bands // pw_size
    chunks = bands // WIDTH
    strip = WIDTH // zsize
    wide = 2 * WIDTH
    half = bands // 2
    piece = half // zsize
    reach = zsize // 2
    any_space = pl.BlockSpec(memory_space=pl.ANY)
    lines = pl.pallas_call(
        functools.partial(kernel, ka_size, zsize),
        out_shape=jax.ShapeDtypeStruct((2, 2, own, bands), F32),
        in_specs=[any_space, any_space],
        out_specs=pl.BlockSpec(memory_space=pltpu.VMEM),
        scratch_shapes=[
            pltpu.VMEM((3, chunks, 2, WIDTH, waves), BF16),
            pltpu.VMEM((chunks, bands, wide), F32),
            pltpu.VMEM((chunks, chunks, WIDTH, wide), F32),
            pltpu.VMEM((chunks, half, wide), F32),
            pltpu.VMEM((chunks, reach, piece, wide), F32),
            pltpu.VMEM((chunks, reach, piece, wide), F32),
            pltpu.VMEM((chunks, reach, chunks, strip, wide), F32),
            pltpu.VMEM((chunks, reach, chunks, strip, wide), F32),
            pltpu.VMEM((chunks, piece, wide), F32),
            pltpu.VMEM((chunks, 2, chunks, strip // 2, wide), F32),
            pltpu.VMEM((chunks, 2, chunks, strip // 2, wide), F32),
            pltpu.VMEM((chunks, bands, wide), F32),
            pltpu.VMEM((chunks, chunks, WIDTH, wide), F32),
            pltpu.VMEM((4, bands, bands), BF16),
            pltpu.VMEM((bands, 2 * bands), BF16),
            pltpu.VMEM((bands, 2 * bands), BF16),
            pltpu.VMEM((bands, 2 * bands), BF16),
            pltpu.VMEM((bands, 2 * bands), BF16),
            pltpu.VMEM((own, 2 * bands), F32),
            pltpu.VMEM((own, 2 * bands), F32),
            pltpu.VMEM((4 * own, bands), BF16),
            pltpu.SemaphoreType.DMA((4 * chunks,)),
            pltpu.SemaphoreType.DMA((SEMS,)),
            pltpu.SemaphoreType.DMA((SEMS,)),
        ],
        compiler_params=pltpu.CompilerParams(
            collective_id=0, has_side_effects=True, vmem_limit_bytes=56 * 1024 * 1024
        ),
    )(states_re, states_im)
    return jnp.transpose(lines, (0, 2, 1, 3))


def solution(mesh):
    in_specs = (P("ka", None, "pw"), P("ka", None, "pw"))
    out_specs = P("ka", "pw", None, None)
    body = functools.partial(shards, mesh.shape["ka"], mesh.shape["pw"])
    return jax.shard_map(body, mesh=mesh, in_specs=in_specs, out_specs=out_specs, check_vma=False)
```

time: 126 us -> 117 us (0.929)
  Pallas kernels: 124 us -> 116 us
    pallas_call x1, Pallas kernels: 124 us -> 116 us  [shards(): pl.pallas_call(functools.partial(kernel, ka_size, zsize), out_shape=jax.S...]
where the time goes in v3:
time: 117 us
  Pallas kernels  116 us (99%)
  local copies, waits for them, and re-layouts  1.66 us (1%)
    pallas_call x1, Pallas kernels, shards(): pl.pallas_call(functools.partial(kernel, ka_size, zsize), out_shape=jax.S...  116 us

profile of v3, /device:TPU:14, one launch (start us, length us, event | category | flops | bytes accessed | tf_op | source)
XLA Modules:
  0.0 117.4 jit_solution(17601490976515105999)
XLA Ops:
  0.0 115.7 %shard_map.28 = f32[2,2,16,512]{3,2,1,0:T(8,128)} custom-call(bf16[2,512,1024]{2,1,0:T(8,128)(2,1)} %re_hbm.1, bf16[2,512,1024]{2,1,0:T(8,128)(2,1)} %im_hbm.1), custom_call_target="tpu_custom_call" | custom-call | tf_op jit(solution)/shard_map/pallas_call | solution.py:466
  115.7 1.7 %copy.3 = f32[2,16,2,512]{3,2,1,0:T(2,128)} copy(f32[2,16,2,512]{3,1,2,0:T(8,128)} %bitcast.1) | data formatting | bytes 262144 | tf_op jit(solution)/shard_map/transpose | solution.py:501

commit v4 on v3

--- a/solution.py
+++ b/solution.py
@@ -52,7 +52,7 @@
     strip = WIDTH // zsize
     thin = strip // 2
     reach = zsize // 2
-    own = rows_in.shape[0]
+    own = rows_in.shape[1]
 
     ka = lax.axis_index("ka")
     pw = lax.axis_index("pw")
@@ -395,49 +395,63 @@
             for chunk in range(chunks):
                 heapq.heappush(order, (when + SPREAD_PACE * chunk, 100 + chunk, "spread", spread(chunk)))
 
-    def apply(high_ref, low_ref):
-        left = stack[...]
+    def keep(h, value):
+        high, low = high_low(value)
+        stack[h] = jnp.concatenate([high[:, :half], low[:, :half], high[:, half:], low[:, half:]], 0)
+
+    def product(high_ref, low_ref, h, chunk):
+        deep, both = pl.ds(h * half, half), pl.ds(chunk * wide, wide)
+        left = stack[h]
         short = jnp.concatenate([left[:own], left[2 * own:3 * own]], 0)
-        pieces_re, pieces_im = [], []
-        for chunk in range(chunks):
-            both = pl.ds(chunk * wide, wide)
-            with_high = dot(left, high_ref[:, both])
-            with_low = dot(short, low_ref[:, both])
-            by_re = with_high[:own] + (with_high[own:2 * own] + with_low[:own])
-            by_im = with_high[2 * own:3 * own] + (with_high[3 * own:] + with_low[own:])
-            pieces_re.append(by_re[:, :WIDTH] - by_im[:, WIDTH:])
-            pieces_im.append(by_re[:, WIDTH:] + by_im[:, :WIDTH])
-        return jnp.concatenate(pieces_re, 1), jnp.concatenate(pieces_im, 1)
-
-    handed = prepare(rows_out, rows_in, to_next)
+        with_high = dot(left, high_ref[deep, both])
+        with_low = dot(short, low_ref[deep, both])
+        by_re = with_high[:own] + (with_high[own:2 * own] + with_low[:own])
+        by_im = with_high[2 * own:3 * own] + (with_high[3 * own:] + with_low[own:])
+        return by_re[:, :WIDTH] - by_im[:, WIDTH:], by_re[:, WIDTH:] + by_im[:, :WIDTH]
+
+    handed = [prepare(rows_out.at[h], rows_in.at[h], to_next) for h in range(2)]
 
     @pl.when(ka == 0)
     def _():
-        row = lax.broadcasted_iota(jnp.int32, (own, 2 * bands), 0) + pw * own
-        column = lax.broadcasted_iota(jnp.int32, (own, 2 * bands), 1)
-        one = (row == column).astype(F32)
-        high, low = high_low(one)
-        stack[...] = jnp.concatenate([high[:, :bands], low[:, :bands], high[:, bands:], low[:, bands:]], 0)
+        for h in range(2):
+            row = lax.broadcasted_iota(jnp.int32, (own, bands), 0) + pw * own
+            column = lax.broadcasted_iota(jnp.int32, (own, bands), 1)
+            keep(h, ((row == column + h * half) & (column < half)).astype(F32))
 
     @pl.when(ka > 0)
     def _():
-        handed.wait_recv()
-        high, low = high_low(rows_in[...])
-        stack[...] = jnp.concatenate([high[:, :bands], low[:, :bands], high[:, bands:], low[:, bands:]], 0)
-
-    line_re, line_im = apply(p_high, p_low)
-    rows_out[:, :bands] = line_re
-    rows_out[:, bands:] = line_im
-
-    @pl.when(ka < ka_size - 1)
+        handed[0].wait_recv()
+        keep(0, rows_in[0])
+
+    begun = [product(p_high, p_low, 0, chunk) for chunk in range(chunks)]
+
+    @pl.when(ka > 0)
     def _():
-        handed.start()
-
-    out_ref[1, 0] = line_re
-    out_ref[1, 1] = line_im
-    line_re, line_im = apply(m0_high, m0_low)
-    out_ref[0, 0] = line_re
-    out_ref[0, 1] = line_im
+        handed[1].wait_recv()
+        keep(1, rows_in[1])
+
+    each = chunks // 2
+    for h in range(2):
+        for n in range(each):
+            chunk = h * each + n
+            more_re, more_im = product(p_high, p_low, 1, chunk)
+            rows_out[h, :, pl.ds(n * WIDTH, WIDTH)] = begun[chunk][0] + more_re
+            rows_out[h, :, pl.ds(half + n * WIDTH, WIDTH)] = begun[chunk][1] + more_im
+
+        @pl.when(ka < ka_size - 1)
+        def _():
+            handed[h].start()
+
+    for h in range(2):
+        columns = pl.ds(h * half, half)
+        out_ref[1, 0, :, columns] = rows_out[h, :, :half]
+        out_ref[1, 1, :, columns] = rows_out[h, :, half:]
+    for chunk in range(chunks):
+        columns = pl.ds(chunk * WIDTH, WIDTH)
+        first_re, first_im = product(m0_high, m0_low, 0, chunk)
+        more_re, more_im = product(m0_high, m0_low, 1, chunk)
+        out_ref[0, 0, :, columns] = first_re + more_re
+        out_ref[0, 1, :, columns] = first_im + more_im
 
     for made in started + joined:
         made.wait_send()
@@ -449,7 +463,8 @@
 
     @pl.when(ka < ka_size - 1)
     def _():
-        handed.wait_send()
+        for made in handed:
+            made.wait_send()
 
 
 def shards(ka_size, pw_size, states_re, states_im):
@@ -487,9 +502,9 @@
             pltpu.VMEM((bands, 2 * bands), BF16),
             pltpu.VMEM((bands, 2 * bands), BF16),
             pltpu.VMEM((bands, 2 * bands), BF16),
-            pltpu.VMEM((own, 2 * bands), F32),
-            pltpu.VMEM((own, 2 * bands), F32),
-            pltpu.VMEM((4 * own, bands), BF16),
+            pltpu.VMEM((2, own, bands), F32),
+            pltpu.VMEM((2, own, bands), F32),
+            pltpu.VMEM((2, 4 * own, half), BF16),
             pltpu.SemaphoreType.DMA((4 * chunks,)),
             pltpu.SemaphoreType.DMA((SEMS,)),
             pltpu.SemaphoreType.DMA((SEMS,)),

time: 117 us -> 116 us (level)
  Pallas kernels: 116 us -> 114 us
    pallas_call x1, Pallas kernels: 116 us -> 114 us  [shards(): pl.pallas_call(functools.partial(kernel, ka_size, zsize), out_shape=jax.S...]
where the time goes in v4:
time: 116 us
  Pallas kernels  114 us (98%)
  local copies, waits for them, and re-layouts  1.66 us (1%)
    pallas_call x1, Pallas kernels, shards(): pl.pallas_call(functools.partial(kernel, ka_size, zsize), out_shape=jax.S...  114 us

profile of v4, /device:TPU:14, one launch (start us, length us, event | category | flops | bytes accessed | tf_op | source)
XLA Modules:
  0.0 115.8 jit_solution(4537294300066501893)
XLA Ops:
  0.0 114.1 %shard_map.28 = f32[2,2,16,512]{3,2,1,0:T(8,128)} custom-call(bf16[2,512,1024]{2,1,0:T(8,128)(2,1)} %re_hbm.1, bf16[2,512,1024]{2,1,0:T(8,128)(2,1)} %im_hbm.1), custom_call_target="tpu_custom_call" | custom-call | tf_op jit(solution)/shard_map/pallas_call | solution.py:481
  114.1 1.7 %copy.3 = f32[2,16,2,512]{3,2,1,0:T(2,128)} copy(f32[2,16,2,512]{3,1,2,0:T(8,128)} %bitcast.1) | data formatting | bytes 262144 | tf_op jit(solution)/shard_map/transpose | solution.py:516

commit v5 on v4

--- a/solution.py
+++ b/solution.py
@@ -14,7 +14,7 @@
 SEMS = 256
 DEPTH = 2
 FIRST_START = 2.0
-FIRST_PACE = 1.5
+FIRST_PACE = 0.8
 GATHER_START = 32.0
 SPREAD_PACE = 1.5
 IN_TWO = (0, 1, 2, 3)

time: 116 us -> 116 us (level)
  no operation moved by 1% of the time
where the time goes in v5:
time: 116 us
  Pallas kernels  114 us (98%)
  local copies, waits for them, and re-layouts  1.66 us (1%)
    pallas_call x1, Pallas kernels, shards(): pl.pallas_call(functools.partial(kernel, ka_size, zsize), out_shape=jax.S...  114 us

profile of v5, /device:TPU:14, one launch (start us, length us, event | category | flops | bytes accessed | tf_op | source)
XLA Modules:
  0.0 116.1 jit_solution(3619386888871426064)
XLA Ops:
  0.0 114.4 %shard_map.28 = f32[2,2,16,512]{3,2,1,0:T(8,128)} custom-call(bf16[2,512,1024]{2,1,0:T(8,128)(2,1)} %re_hbm.1, bf16[2,512,1024]{2,1,0:T(8,128)(2,1)} %im_hbm.1), custom_call_target="tpu_custom_call" | custom-call | tf_op jit(solution)/shard_map/pallas_call | solution.py:481
  114.4 1.7 %copy.3 = f32[2,16,2,512]{3,2,1,0:T(2,128)} copy(f32[2,16,2,512]{3,1,2,0:T(8,128)} %bitcast.1) | data formatting | bytes 262144 | tf_op jit(solution)/shard_map/transpose | solution.py:516
